TPU v7x, 32 devices: a whole 2x2x4 slice. The times are simulated.
32 devices in a mesh: dp: 8 (over z, y), expert: 4 (over x, core).
Axes of the slice: x: 2, y: 2, z: 4, core: 2. Of those that a mesh axis runs over, the one named last changes fastest.
Arguments:
- tokens: bfloat16 [4096, 2048], P(('dp', 'expert')), may hold values from -6 to 6
- routes: int32 [4096, 8], P(('dp', 'expert')), may hold values from 0 to 15, all different within a row; in each aligned block of 128 rows (0 to 127, 128 to 255, ...) at most 80 rows name the same one
- gates: bfloat16 [4096, 8], P(('dp', 'expert')), may hold values from 0.099609375 to 0.5
- cotangent: bfloat16 [4096, 2048], P(('dp', 'expert')), may hold values from -6 to 6
- w_gate: bfloat16 [16, 2048, 384], P('dp'), may hold values from -0.125 to 0.125
- w_up: bfloat16 [16, 2048, 384], P('dp'), may hold values from -0.125 to 0.125
- w_down: bfloat16 [16, 384, 2048], P('dp'), may hold values from -0.3125 to 0.3125
Outputs:
- layer_out: bfloat16 [4096, 2048], P(('dp', 'expert'))
- grad_tokens: bfloat16 [4096, 2048], P(('dp', 'expert'))
- grad_gate: bfloat16 [16, 2048, 384], P('dp', 'expert')
- grad_up: bfloat16 [16, 2048, 384], P('dp', 'expert')
- grad_down: bfloat16 [16, 384, 2048], P('dp', None, 'expert')
Inputs may be any that keep to these rules, and one draw needn't show every extreme that they name: `routes`: each row names 8 different experts. Among the rows of one device, no expert is named by more than 80 rows, and in every draw some device has an expert named by exactly 80 rows.
All inputs are finite; a program needn't handle non-finite values.
Results may differ from a plain program's by a relative error of at most 0.012.
Values may be sent and summed in bfloat16 or wider, within the bound.
A program may use at most 128 MiB of HBM per device.

v0:
```python
import jax
import jax.numpy as jnp
from jax import lax
from jax.sharding import PartitionSpec as P


def expert_forward(arrived, w_gate, w_up, w_down):
    gate_act = jnp.einsum("erd,edf->erf", arrived, w_gate, preferred_element_type=jnp.float32)
    up_act = jnp.einsum("erd,edf->erf", arrived, w_up, preferred_element_type=jnp.float32)
    sigma_gate = jax.nn.sigmoid(gate_act)
    smooth = gate_act * sigma_gate
    hidden = (smooth * up_act).astype(jnp.bfloat16)
    result = jnp.einsum("erf,efd->erd", hidden, w_down, preferred_element_type=jnp.float32).astype(
        jnp.bfloat16
    )
    return (gate_act, up_act, sigma_gate, smooth, hidden, result)


def body(tokens, routes, gates, cotangent, w_gate, w_up, w_down):
    tok_rows, top_k = routes.shape
    width = tokens.shape[1]
    owners = lax.axis_size("dp")
    per_owner = w_gate.shape[0]
    hidden_units = w_gate.shape[2]
    experts = owners * per_owner
    capacity = max(2, tok_rows * top_k * 5 // (4 * experts))
    slot_count = experts * capacity
    chosen = routes.reshape(-1)
    onehot = (chosen[:, None] == jnp.arange(experts, dtype=jnp.int32)[None, :]).astype(jnp.int32)
    order_in = jnp.sum((jnp.cumsum(onehot, axis=0) - onehot) * onehot, axis=1)
    slot_index = chosen * capacity + order_in
    token_of = jnp.arange(tok_rows * top_k, dtype=jnp.int32) // top_k
    table = jnp.full((slot_count,), tok_rows, jnp.int32).at[slot_index].set(token_of)
    slot_gain = (
        jnp.zeros((slot_count,), jnp.float32)
        .at[slot_index]
        .set(gates.reshape(-1).astype(jnp.float32))
    )
    padded_x = jnp.concatenate([tokens, jnp.zeros((1, width), tokens.dtype)], axis=0)
    padded_c = jnp.concatenate([cotangent, jnp.zeros((1, width), cotangent.dtype)], axis=0)
    send_rows = padded_x[table].reshape(experts, capacity, width)
    send_grads = (slot_gain[:, None] * padded_c[table].astype(jnp.float32)).astype(jnp.bfloat16)
    send_grads = send_grads.reshape(experts, capacity, width)
    arrived = lax.all_to_all(send_rows, "dp", split_axis=0, concat_axis=1, tiled=True)
    state = expert_forward(arrived, w_gate, w_up, w_down)
    arrived_grad = lax.all_to_all(send_grads, "dp", split_axis=0, concat_axis=1, tiled=True)
    gate_act, up_act, sigma_gate, smooth, hidden, result = state
    returned = lax.all_to_all(result, "dp", split_axis=1, concat_axis=0, tiled=True).reshape(
        slot_count, width
    )
    picked = returned[slot_index].reshape(tok_rows, top_k, width)
    layer_out = jnp.einsum("tk,tkd->td", gates, picked, preferred_element_type=jnp.float32).astype(
        jnp.bfloat16
    )
    grad_hidden = jnp.einsum(
        "erd,efd->erf", arrived_grad, w_down, preferred_element_type=jnp.float32
    )
    grad_upact = (grad_hidden * smooth).astype(jnp.bfloat16)
    grad_gateact = (
        grad_hidden * up_act * sigma_gate * (1.0 + gate_act * (1.0 - sigma_gate))
    ).astype(jnp.bfloat16)
    row_grads = (
        jnp.einsum("erf,edf->erd", grad_gateact, w_gate, preferred_element_type=jnp.float32)
        + jnp.einsum("erf,edf->erd", grad_upact, w_up, preferred_element_type=jnp.float32)
    ).astype(jnp.bfloat16)
    came_back = lax.all_to_all(row_grads, "dp", split_axis=1, concat_axis=0, tiled=True).reshape(
        slot_count, width
    )
    grad_picked = came_back[slot_index].reshape(tok_rows, top_k, width)
    grad_tokens = jnp.sum(grad_picked.astype(jnp.float32), axis=1).astype(jnp.bfloat16)
    both_factors = jnp.concatenate([grad_gateact, grad_upact], axis=2)
    input_term = jnp.einsum(
        "erd,erf->def", arrived, both_factors, preferred_element_type=jnp.float32
    )
    down_term = jnp.einsum("erf,erd->def", hidden, arrived_grad, preferred_element_type=jnp.float32)
    totals = lax.psum_scatter(
        jnp.concatenate([input_term, down_term], axis=2).astype(jnp.bfloat16),
        "expert",
        scatter_dimension=0,
        tiled=True,
    ).astype(jnp.float32)
    grad_gate = jnp.transpose(totals[:, :, :hidden_units], (1, 0, 2)).astype(jnp.bfloat16)
    grad_up = jnp.transpose(totals[:, :, hidden_units : 2 * hidden_units], (1, 0, 2)).astype(
        jnp.bfloat16
    )
    grad_down = jnp.transpose(totals[:, :, 2 * hidden_units :], (1, 2, 0)).astype(jnp.bfloat16)
    return (layer_out, grad_tokens, grad_gate, grad_up, grad_down)


def solution(mesh):
    return jax.shard_map(
        body,
        mesh=mesh,
        in_specs=(
            P(("dp", "expert"), None),
            P(("dp", "expert"), None),
            P(("dp", "expert"), None),
            P(("dp", "expert"), None),
            P("dp", None, None),
            P("dp", None, None),
            P("dp", None, None),
        ),
        out_specs=(
            P(("dp", "expert"), None),
            P(("dp", "expert"), None),
            P("dp", "expert", None),
            P("dp", "expert", None),
            P("dp", None, "expert"),
        ),
        check_vma=False,
    )
```

profile of v0, /device:TPU:0, one launch (start us, length us, event | category | flops | bytes accessed | tf_op | source)
XLA Modules:
  0.0 627.4 jit_solution(449941669003016595)
XLA Ops:
  7.2 0.9 copy.41
  8.1 0.1 eq.29
  8.3 0.7 broadcast_multiply_fusion
  9.0 4.5 reduce-window.6
  13.6 0.1 copy.43
  13.9 0.1 copy.40
  14.0 0.1 mul.53
  14.2 4.3 scatter_custom_fusion
  18.5 0.8 copy.51
  19.4 4.3 scatter_custom_fusion.1
  23.8 1.9 concatenate.14
  25.7 11.9 %gather_fusion.2 = bf16[1280,2048]{1,0:T(8,128)(2,1)} fusion(bf16[129,2048]{1,0:T(8,128)(2,1)} %concatenate.14, s32[2048]{0:T(1024)S(1)} %pad_clamp_fusion), kind=kCustom, calls=%fused_computation.2 | custom fusion | bytes 10490880 | tf_op jit(solution)/shard_map/gather | solution.py:42
  37.7 5.7 fusion
  43.4 7.3 %all-to-all-start.2 = ((bf16[16,80,2048]{2,1,0:T(8,128)(2,1)}), bf16[16,80,2048]{2,1,0:T(8,128)(2,1)}, u32[]{:S(2)}, u32[]{:S(2)}) async-start(bf16[16,80,2048]{2,1,0:T(8,128)(2,1)} %fusion), calls=%async_computation.2 | async-start | bytes 10485760 | tf_op jit(solution)/shard_map/all_to_all | solution.py:46
  50.7 1.9 concatenate.13
  52.6 12.0 %gather_fusion = bf16[1280,2048]{1,0:T(8,128)(2,1)} fusion(bf16[129,2048]{1,0:T(8,128)(2,1)} %concatenate.13, s32[2048]{0:T(1024)S(1)} %pad_clamp_fusion), kind=kCustom, calls=%fused_computation | custom fusion | bytes 10490880 | tf_op jit(solution)/shard_map/gather | solution.py:41
  64.5 101.9 %all-to-all-done.2 = bf16[16,80,2048]{2,1,0:T(8,128)(2,1)} async-done(((bf16[16,80,2048]{2,1,0:T(8,128)(2,1)}), bf16[16,80,2048]{2,1,0:T(8,128)(2,1)}, u32[]{:S(2)}, u32[]{:S(2)}) %all-to-all-start.2) | async-done | bytes 5242912 | tf_op jit(solution)/shard_map/all_to_all | solution.py:46
  166.4 4.8 all-to-all-start
  171.3 5.6 copy.52
  176.9 109.3 %all-to-all-done = bf16[16,80,2048]{2,1,0:T(8,128)(2,1)} async-done(((bf16[16,80,2048]{2,1,0:T(8,128)(2,1)}), bf16[16,80,2048]{2,1,0:T(8,128)(2,1)}, u32[]{:S(2)}, u32[]{:S(2)}) %all-to-all-start) | async-done | bytes 5242912 | tf_op jit(solution)/shard_map/all_to_all | solution.py:44
  286.2 3.1 copy.45
  289.3 0.3 copy-done.4
  289.6 4.2 fusion.20
  293.8 4.1 fusion.21
  297.9 6.0 multiply_convert_fusion
  303.9 3.1 fusion.22
  307.1 7.1 %convert_bitcast_fusion = bf16[2048,2,768]{0,2,1:T(8,128)(2,1)} fusion(bf16[2,640,2048]{2,1,0:T(8,128)(2,1)S(1)} %bitcast.86, bf16[2,640,384]{1,2,0:T(8,128)(2,1)S(1)} %copy-done.7, bf16[2,640,384]{1,2,0:T(8,128)(2,1)S(1)} %get-tuple-element.21), kind=kOutput, calls=%fused_computation.10 | convolution fusion | flops 4033609728 | bytes 13500416 | tf_op jit(solution)/shard_map/erd,erf->def/dot_general | solution.py:72
  314.3 4.0 fusion.3
  318.2 5.2 add_convert_fusion
  323.4 10.2 %copy.55 = bf16[2,640,2048]{2,0,1:T(2,128)(2,1)} copy(bf16[2,640,2048]{2,1,0:T(8,128)(2,1)} %add_convert_fusion) | data formatting | bytes 10485760 | tf_op jit(solution)/shard_map/convert_element_type | solution.py:65
  333.6 4.7 all-to-all-start.3
  338.4 8.2 %pad_maximum_fusion = bf16[2048,2,1152]{0,2,1:T(8,128)(2,1)} fusion(bf16[2048,2,384]{0,2,1:T(8,128)(2,1)} %fusion.3, bf16[2048,2,768]{0,2,1:T(8,128)(2,1)} %convert_bitcast_fusion), kind=kLoop, calls=%fused_computation.9 | loop fusion | flops 18874368 | bytes 18874368 | tf_op jit(solution)/shard_map/concatenate | solution.py:77
  346.6 5.9 convolution_convert_fusion
  352.6 11.0 %copy.49 = bf16[2,640,2048]{2,0,1:T(2,128)(2,1)} copy(bf16[2,640,2048]{2,1,0:T(8,128)(2,1)} %convolution_convert_fusion) | data formatting | bytes 10485760 | tf_op jit(solution)/shard_map/convert_element_type | solution.py:13
  363.6 89.6 %all-to-all-done.3 = bf16[2,640,2048]{2,0,1:T(2,128)(2,1)} async-done(((bf16[2,640,2048]{2,0,1:T(2,128)(2,1)}), bf16[2,640,2048]{2,0,1:T(2,128)(2,1)}, u32[]{:S(2)}, u32[]{:S(2)}) %all-to-all-start.3) | async-done | bytes 5242912 | tf_op jit(solution)/shard_map/all_to_all | solution.py:66
  453.2 4.8 all-to-all-start.1
  458.0 0.1 copy.62
  458.2 7.2 %copy.56 = bf16[2,8,80,2048]{3,2,0,1:T(8,128)(2,1)} copy(bf16[2,8,80,2048]{3,0,2,1:T(2,128)(2,1)} %bitcast.18) | data formatting | bytes 10485760 | tf_op jit(solution)/shard_map/all_to_all | solution.py:66
  465.4 107.5 %all-to-all-done.1 = bf16[2,640,2048]{2,0,1:T(2,128)(2,1)} async-done(((bf16[2,640,2048]{2,0,1:T(2,128)(2,1)}), bf16[2,640,2048]{2,0,1:T(2,128)(2,1)}, u32[]{:S(2)}, u32[]{:S(2)}) %all-to-all-start.1) | async-done | bytes 5242912 | tf_op jit(solution)/shard_map/all_to_all | solution.py:48
  572.9 7.3 %copy.50 = bf16[2,8,80,2048]{3,2,0,1:T(8,128)(2,1)} copy(bf16[2,8,80,2048]{3,0,2,1:T(2,128)(2,1)} %bitcast.8) | data formatting | bytes 10485760 | tf_op jit(solution)/shard_map/all_to_all | solution.py:48
  580.2 12.0 %gather_fusion.3 = bf16[1024,2048]{1,0:T(8,128)(2,1)} fusion(bf16[1280,2048]{1,0:T(8,128)(2,1)} %bitcast.74, s32[1024]{0:T(1024)S(1)} %broadcast_clamp_fusion), kind=kCustom, calls=%fused_computation.3 | custom fusion | bytes 8392704 | tf_op jit(solution)/shard_map/gather | solution.py:69
  592.2 12.2 %gather_fusion.1 = bf16[1024,2048]{1,0:T(8,128)(2,1)} fusion(bf16[1280,2048]{1,0:T(8,128)(2,1)} %bitcast.75, s32[1024]{0:T(1024)S(1)} %broadcast_clamp_fusion), kind=kCustom, calls=%fused_computation.1 | custom fusion | bytes 8392704 | tf_op jit(solution)/shard_map/gather | solution.py:51
  604.3 3.6 fusion.1
  607.9 1.1 copy.69
  609.0 3.7 bitcast_reduce_fusion
  612.7 3.1 slice_bitcast_fusion
  615.7 2.3 copy.57
  618.0 2.3 copy.58
  (49 shorter events, 0.7 us)
Async XLA Ops:
  7.2 290.7 %copy-start = (bf16[2,384,2048]{2,1,0:T(8,128)(2,1)S(1)}, bf16[2,384,2048]{2,1,0:T(8,128)(2,1)}, u32[]{:S(2)}) copy-start(bf16[2,384,2048]{2,1,0:T(8,128)(2,1)} %param.13) | copy-start | bytes 9437188
  43.4 123.1 %all-to-all-start.2 = ((bf16[16,80,2048]{2,1,0:T(8,128)(2,1)}), bf16[16,80,2048]{2,1,0:T(8,128)(2,1)}, u32[]{:S(2)}, u32[]{:S(2)}) async-start(bf16[16,80,2048]{2,1,0:T(8,128)(2,1)} %fusion), calls=%async_computation.2 | async-start | bytes 10485760 | tf_op jit(solution)/shard_map/all_to_all | solution.py:46
  166.4 119.7 %all-to-all-start = ((bf16[16,80,2048]{2,1,0:T(8,128)(2,1)}), bf16[16,80,2048]{2,1,0:T(8,128)(2,1)}, u32[]{:S(2)}, u32[]{:S(2)}) async-start(bf16[16,80,2048]{2,1,0:T(8,128)(2,1)} %bitcast.76), calls=%async_computation | async-start | bytes 10485760 | tf_op jit(solution)/shard_map/all_to_all | solution.py:44
  286.2 3.4 copy-start.4
  289.3 4.5 copy-start.2
  289.6 4.2 copy-start.5
  289.6 8.3 %slice-start = ((s8[5242880]{0:T(1024)(128)(4,1)}), s8[4194304]{0:T(1024)(128)(4,1)S(1)}, s32[]{:S(2)}) async-start(s8[5242880]{0:T(1024)(128)(4,1)} %bitcast.78), calls=%async_computation.6 | async-start | bytes 8388608
  293.8 4.1 slice-start.1
  303.9 3.2 copy-start.3
  303.9 3.2 copy-start.7
  303.9 10.3 %slice-start.2 = ((s8[5242880]{0:T(1024)(128)(4,1)}), s8[4194304]{0:T(1024)(128)(4,1)S(1)}, s32[]{:S(2)}) async-start(s8[5242880]{0:T(1024)(128)(4,1)} %bitcast.81), calls=%async_computation.8 | async-start | bytes 8388608
  307.1 7.2 %slice-start.3 = ((s8[5242880]{0:T(1024)(128)(4,1)}), s8[1048576]{0:T(1024)(128)(4,1)S(1)}, s32[]{:S(2)}) async-start(s8[5242880]{0:T(1024)(128)(4,1)} %bitcast.81), calls=%async_computation.9 | async-start | bytes 2097152
  307.1 7.1 %copy-start.10 = (bf16[2,640,384]{1,2,0:T(8,128)(2,1)S(1)}, bf16[2,640,384]{1,2,0:T(8,128)(2,1)}, u32[]{:S(2)}) copy-start(bf16[2,640,384]{1,2,0:T(8,128)(2,1)} %get-tuple-element.22) | copy-start | bytes 2949124
  314.2 4.0 copy-start.6
  314.2 4.0 copy-start.8
  333.6 119.6 %all-to-all-start.3 = ((bf16[2,640,2048]{2,0,1:T(2,128)(2,1)}), bf16[2,640,2048]{2,0,1:T(2,128)(2,1)}, u32[]{:S(2)}, u32[]{:S(2)}) async-start(bf16[2,640,2048]{2,0,1:T(2,128)(2,1)} %copy.55), calls=%async_computation.3 | async-start | bytes 10485760 | tf_op jit(solution)/shard_map/all_to_all | solution.py:66
  338.4 274.3 %reduce-scatter.2.cloned.1.call-start = ((), (), s32[]{:S(2)}) async-start(), calls=%async_computation.5 | async-start | bytes 11796480 | tf_op jit(solution)/shard_map/reduce_scatter | solution.py:76
  363.6 94.4 %copy-start.9 = (bf16[128,8]{0,1:T(8,128)(2,1)S(1)}, bf16[128,8]{0,1:T(8,128)(2,1)}, u32[]{:S(2)}) copy-start(bf16[128,8]{0,1:T(8,128)(2,1)} %param.9) | copy-start | bytes 6148
  453.2 119.7 %all-to-all-start.1 = ((bf16[2,640,2048]{2,0,1:T(2,128)(2,1)}), bf16[2,640,2048]{2,0,1:T(2,128)(2,1)}, u32[]{:S(2)}, u32[]{:S(2)}) async-start(bf16[2,640,2048]{2,0,1:T(2,128)(2,1)} %copy.49), calls=%async_computation.1 | async-start | bytes 10485760 | tf_op jit(solution)/shard_map/all_to_all | solution.py:48
  604.3 4.7 copy-start.1
Sparse Core Ops, SparseCore 0:
  346.8 79.0 reduce-scatter.1
where the time goes:
time: 635 us; the launch traced here: 627 us
  waiting for transfers between devices  408 us (64%)
  local copies, waits for them, and re-layouts  117 us (18%)
  matrix products  43.2 us (7%)
  other arithmetic  23 us (4%)
  starting transfers between devices  21.7 us (3%)
  between operations  14.5 us (2%)
    all_to_all x1, waiting for transfers between devices, body(): lax.all_to_all(send_rows, 'dp', split_axis=0, concat_axis=1, tiled=True)  109 us
    all_to_all x1, waiting for transfers between devices, body(): lax.all_to_all(result, 'dp', split_axis=1, concat_axis=0, tiled=True)  108 us
    all_to_all x1, waiting for transfers between devices, body(): lax.all_to_all(send_grads, 'dp', split_axis=0, concat_axis=1, tiled=True)  102 us
    all_to_all x1, waiting for transfers between devices, body(): lax.all_to_all(row_grads, 'dp', split_axis=1, concat_axis=0, tiled=True)  89.6 us
  transfers between devices with their start and end apart: 5, of which 4 were waited for; matrix products, arithmetic and copies ran while one was open for 15% of the time, Pallas kernels for 0%

commit v1 on v0

--- a/solution.py
+++ b/solution.py
@@ -2,6 +2,7 @@
 import jax.numpy as jnp
 from jax import lax
 from jax.sharding import PartitionSpec as P
+from jax.lax import all_to_all, axis_size
 
 
 def expert_forward(arrived, w_gate, w_up, w_down):
@@ -63,9 +64,16 @@
         jnp.einsum("erf,edf->erd", grad_gateact, w_gate, preferred_element_type=jnp.float32)
         + jnp.einsum("erf,edf->erd", grad_upact, w_up, preferred_element_type=jnp.float32)
     ).astype(jnp.bfloat16)
-    came_back = lax.all_to_all(row_grads, "dp", split_axis=1, concat_axis=0, tiled=True).reshape(
-        slot_count, width
+    area_play = lambda frame_in, comm_axis: jnp.concatenate(
+        all_to_all(
+            jnp.stack(jnp.split(frame_in, axis_size(comm_axis), axis=1)),
+            comm_axis,
+            split_axis=0,
+            concat_axis=0,
+        ),
+        axis=0,
     )
+    came_back = area_play(row_grads, "dp").reshape(slot_count, width)
     grad_picked = came_back[slot_index].reshape(tok_rows, top_k, width)
     grad_tokens = jnp.sum(grad_picked.astype(jnp.float32), axis=1).astype(jnp.bfloat16)
     both_factors = jnp.concatenate([grad_gateact, grad_upact], axis=2)

time: 635 us -> 614 us (0.967)
  waiting for transfers between devices: 408 us -> 389 us
    all_to_all x1, waiting for transfers between devices: 108 us -> 70.2 us  [body(): lax.all_to_all(result, 'dp', split_axis=1, concat_axis=0, tiled=True)]
    all_to_all x1, waiting for transfers between devices: 89.6 us -> 108 us  [body(): all_to_all(jnp.stack(jnp.split(frame_in, axis_size(comm_axis), axis=1)),...]
    unnamed x34 -> x37, local copies, waits for them, and re-layouts: 6.04 us -> 23 us
    convert_element_type x1 -> x0, local copies, waits for them, and re-layouts: 10.2 us -> none  [body(): row_grads = (jnp.einsum('erf,edf->erd', grad_gateact, w_gate, preferred_e...]
    all_to_all x1 -> x0, local copies, waits for them, and re-layouts: 7.24 us -> none  [body(): lax.all_to_all(row_grads, 'dp', split_axis=1, concat_axis=0, tiled=True)]
  transfers between devices with their start and end apart: 5 -> 5, of which waited for: 4 -> 4; matrix products, arithmetic and copies ran while one was open for 15% -> 17% of each run, Pallas kernels for 0% -> 0%
where the time goes in v1:
time: 614 us; the launch traced here: 607 us
  waiting for transfers between devices  389 us (63%)
  local copies, waits for them, and re-layouts  117 us (19%)
  matrix products  40.5 us (7%)
  other arithmetic  23.3 us (4%)
  starting transfers between devices  22 us (4%)
  between operations  14.5 us (2%)
    all_to_all x1, waiting for transfers between devices, body(): lax.all_to_all(send_rows, 'dp', split_axis=0, concat_axis=1, tiled=True)  109 us
    all_to_all x1, waiting for transfers between devices, body(): all_to_all(jnp.stack(jnp.split(frame_in, axis_size(comm_axis), axis=1)),...  108 us
    all_to_all x1, waiting for transfers between devices, body(): lax.all_to_all(send_grads, 'dp', split_axis=0, concat_axis=1, tiled=True)  102 us
    all_to_all x1, waiting for transfers between devices, body(): lax.all_to_all(result, 'dp', split_axis=1, concat_axis=0, tiled=True)  70.2 us
    unnamed x37, local copies, waits for them, and re-layouts  23 us
  transfers between devices with their start and end apart: 5, of which 4 were waited for; matrix products, arithmetic and copies ran while one was open for 17% of the time, Pallas kernels for 0%

profile of v1, /device:TPU:0, one launch (start us, length us, event | category | flops | bytes accessed | tf_op | source)
XLA Modules:
  0.0 606.6 jit_solution(9786638141905217063)
XLA Ops:
  7.2 0.9 copy.39
  9.0 4.5 reduce-window.6
  14.2 4.3 scatter_custom_fusion
  18.5 0.8 copy.49
  19.4 4.3 scatter_custom_fusion.1
  23.8 1.9 concatenate.14
  25.7 11.9 %gather_fusion.2 = bf16[1280,2048]{1,0:T(8,128)(2,1)} fusion(bf16[129,2048]{1,0:T(8,128)(2,1)} %concatenate.14, s32[2048]{0:T(1024)S(1)} %pad_clamp_fusion), kind=kCustom, calls=%fused_computation.2 | custom fusion | bytes 10490880 | tf_op jit(solution)/shard_map/gather | solution.py:43
  37.7 5.8 fusion
  43.4 7.3 %all-to-all-start.2 = ((bf16[16,80,2048]{2,1,0:T(8,128)(2,1)}), bf16[16,80,2048]{2,1,0:T(8,128)(2,1)}, u32[]{:S(2)}, u32[]{:S(2)}) async-start(bf16[16,80,2048]{2,1,0:T(8,128)(2,1)} %fusion), calls=%async_computation.2 | async-start | bytes 10485760 | tf_op jit(solution)/shard_map/all_to_all | solution.py:47
  50.7 1.9 concatenate.13
  52.6 11.9 %gather_fusion = bf16[1280,2048]{1,0:T(8,128)(2,1)} fusion(bf16[129,2048]{1,0:T(8,128)(2,1)} %concatenate.13, s32[2048]{0:T(1024)S(1)} %pad_clamp_fusion), kind=kCustom, calls=%fused_computation | custom fusion | bytes 10490880 | tf_op jit(solution)/shard_map/gather | solution.py:42
  64.6 101.9 %all-to-all-done.2 = bf16[16,80,2048]{2,1,0:T(8,128)(2,1)} async-done(((bf16[16,80,2048]{2,1,0:T(8,128)(2,1)}), bf16[16,80,2048]{2,1,0:T(8,128)(2,1)}, u32[]{:S(2)}, u32[]{:S(2)}) %all-to-all-start.2) | async-done | bytes 5242912 | tf_op jit(solution)/shard_map/all_to_all | solution.py:47
  166.5 5.1 all-to-all-start
  171.6 5.7 copy.50
  177.3 109.2 %all-to-all-done = bf16[16,80,2048]{2,1,0:T(8,128)(2,1)} async-done(((bf16[16,80,2048]{2,1,0:T(8,128)(2,1)}), bf16[16,80,2048]{2,1,0:T(8,128)(2,1)}, u32[]{:S(2)}, u32[]{:S(2)}) %all-to-all-start) | async-done | bytes 5242912 | tf_op jit(solution)/shard_map/all_to_all | solution.py:45
  286.5 3.3 copy.43
  290.0 2.9 fusion.28
  293.6 2.9 fusion.29
  296.5 4.7 multiply_convert_fusion
  301.2 3.9 fusion.3
  305.2 4.9 convolution_convert_fusion
  310.1 10.1 %copy.47 = bf16[2,640,2048]{2,0,1:T(2,128)(2,1)} copy(bf16[2,640,2048]{2,1,0:T(8,128)(2,1)} %convolution_convert_fusion) | data formatting | bytes 10485760 | tf_op jit(solution)/shard_map/convert_element_type | solution.py:14
  320.2 4.7 all-to-all-start.1
  324.9 7.7 %convert_bitcast_fusion = bf16[2048,2,768]{0,2,1:T(8,128)(2,1)S(1)} fusion(bf16[2,640,2048]{2,1,0:T(8,128)(2,1)} %bitcast.108, bf16[2,640,384]{1,2,0:T(8,128)(2,1)} %get-tuple-element.20, bf16[2,640,384]{1,2,0:T(8,128)(2,1)} %get-tuple-element.21), kind=kOutput, calls=%fused_computation.10 | convolution fusion | flops 4033609728 | bytes 13500416 | tf_op jit(solution)/shard_map/erd,erf->def/dot_general | solution.py:80
  332.7 8.5 %pad_maximum_fusion = bf16[2048,2,1152]{0,2,1:T(8,128)(2,1)} fusion(bf16[2048,2,384]{0,2,1:T(8,128)(2,1)S(1)} %copy-done.8, bf16[2048,2,768]{0,2,1:T(8,128)(2,1)S(1)} %convert_bitcast_fusion), kind=kLoop, calls=%fused_computation.9 | loop fusion | flops 18874368 | bytes 18874368 | tf_op jit(solution)/shard_map/concatenate | solution.py:85
  341.2 1.9 copy-done.5
  343.1 4.4 fusion.30
  347.5 5.5 add_convert_fusion
  353.0 2.2 fusion.15
  355.2 2.1 fusion.14
  357.3 2.0 fusion.13
  359.3 2.0 fusion.12
  361.4 2.0 fusion.11
  363.3 2.0 fusion.10
  365.3 2.2 fusion.9
  367.5 2.0 fusion.8
  369.6 70.2 %all-to-all-done.1 = bf16[2,640,2048]{2,0,1:T(2,128)(2,1)} async-done(((bf16[2,640,2048]{2,0,1:T(2,128)(2,1)}), bf16[2,640,2048]{2,0,1:T(2,128)(2,1)}, u32[]{:S(2)}, u32[]{:S(2)}) %all-to-all-start.1) | async-done | bytes 5242912 | tf_op jit(solution)/shard_map/all_to_all | solution.py:49
  439.8 4.9 all-to-all-start.3
  444.8 7.2 %copy.48 = bf16[2,8,80,2048]{3,2,0,1:T(8,128)(2,1)} copy(bf16[2,8,80,2048]{3,0,2,1:T(2,128)(2,1)} %bitcast.8) | data formatting | bytes 10485760 | tf_op jit(solution)/shard_map/all_to_all | solution.py:49
  451.9 107.6 %all-to-all-done.3 = bf16[8,2,80,2048]{3,2,1,0:T(8,128)(2,1)} async-done(((bf16[8,2,80,2048]{3,2,1,0:T(8,128)(2,1)}), bf16[8,2,80,2048]{3,2,1,0:T(8,128)(2,1)}, u32[]{:S(2)}, u32[]{:S(2)}) %all-to-all-start.3) | async-done | bytes 5242912 | tf_op jit(solution)/shard_map/all_to_all | solution.py:68
  559.5 12.0 %gather_fusion.3 = bf16[1024,2048]{1,0:T(8,128)(2,1)} fusion(bf16[1280,2048]{1,0:T(8,128)(2,1)} %bitcast.26, s32[1024]{0:T(1024)S(1)} %broadcast_clamp_fusion), kind=kCustom, calls=%fused_computation.3 | custom fusion | bytes 8392704 | tf_op jit(solution)/shard_map/gather | solution.py:77
  571.5 12.0 %gather_fusion.1 = bf16[1024,2048]{1,0:T(8,128)(2,1)} fusion(bf16[1280,2048]{1,0:T(8,128)(2,1)} %bitcast.103, s32[1024]{0:T(1024)S(1)} %broadcast_clamp_fusion), kind=kCustom, calls=%fused_computation.1 | custom fusion | bytes 8392704 | tf_op jit(solution)/shard_map/gather | solution.py:52
  583.5 3.6 fusion.1
  587.1 1.1 copy.65
  588.2 3.7 bitcast_reduce_fusion
  591.9 3.1 slice_bitcast_fusion
  594.9 2.3 copy.53
  597.2 2.3 copy.54
  (50 shorter events, 2.8 us)
Async XLA Ops:
  7.2 289.3 %copy-start = (bf16[2,384,2048]{2,1,0:T(8,128)(2,1)S(1)}, bf16[2,384,2048]{2,1,0:T(8,128)(2,1)}, u32[]{:S(2)}) copy-start(bf16[2,384,2048]{2,1,0:T(8,128)(2,1)} %param.13) | copy-start | bytes 9437188
  43.4 123.1 %all-to-all-start.2 = ((bf16[16,80,2048]{2,1,0:T(8,128)(2,1)}), bf16[16,80,2048]{2,1,0:T(8,128)(2,1)}, u32[]{:S(2)}, u32[]{:S(2)}) async-start(bf16[16,80,2048]{2,1,0:T(8,128)(2,1)} %fusion), calls=%async_computation.2 | async-start | bytes 10485760 | tf_op jit(solution)/shard_map/all_to_all | solution.py:47
  166.5 120.0 %all-to-all-start = ((bf16[16,80,2048]{2,1,0:T(8,128)(2,1)}), bf16[16,80,2048]{2,1,0:T(8,128)(2,1)}, u32[]{:S(2)}, u32[]{:S(2)}) async-start(bf16[16,80,2048]{2,1,0:T(8,128)(2,1)} %bitcast.104), calls=%async_computation | async-start | bytes 10485760 | tf_op jit(solution)/shard_map/all_to_all | solution.py:45
  286.5 3.4 copy-start.4
  289.8 3.1 copy-start.3
  290.0 3.6 copy-start.6
  290.0 6.5 %slice-start = ((s8[5242880]{0:T(1024)(128)(4,1)}), s8[4194304]{0:T(1024)(128)(4,1)S(1)}, s32[]{:S(2)}) async-start(s8[5242880]{0:T(1024)(128)(4,1)} %bitcast.109), calls=%async_computation.6 | async-start | bytes 8388608
  293.6 2.9 slice-start.1
  320.2 119.6 %all-to-all-start.1 = ((bf16[2,640,2048]{2,0,1:T(2,128)(2,1)}), bf16[2,640,2048]{2,0,1:T(2,128)(2,1)}, u32[]{:S(2)}, u32[]{:S(2)}) async-start(bf16[2,640,2048]{2,0,1:T(2,128)(2,1)} %copy.47), calls=%async_computation.1 | async-start | bytes 10485760 | tf_op jit(solution)/shard_map/all_to_all | solution.py:49
  324.9 267.0 %reduce-scatter.2.cloned.1.call-start = ((), (), s32[]{:S(2)}) async-start(), calls=%async_computation.5 | async-start | bytes 11796480 | tf_op jit(solution)/shard_map/reduce_scatter | solution.py:84
  324.9 7.8 %copy-start.8 = (bf16[2048,2,384]{0,2,1:T(8,128)(2,1)S(1)}, bf16[2048,2,384]{0,2,1:T(8,128)(2,1)}, u32[]{:S(2)}) copy-start(bf16[2048,2,384]{0,2,1:T(8,128)(2,1)} %fusion.3) | copy-start | bytes 9437188
  341.2 1.9 copy-start.5
  343.1 4.4 copy-start.7
  343.1 4.4 copy-start.9
  369.5 75.1 %copy-start.10 = (bf16[128,8]{0,1:T(8,128)(2,1)S(1)}, bf16[128,8]{0,1:T(8,128)(2,1)}, u32[]{:S(2)}) copy-start(bf16[128,8]{0,1:T(8,128)(2,1)} %param.9) | copy-start | bytes 6148
  439.8 119.8 %all-to-all-start.3 = ((bf16[8,2,80,2048]{3,2,1,0:T(8,128)(2,1)}), bf16[8,2,80,2048]{3,2,1,0:T(8,128)(2,1)}, u32[]{:S(2)}, u32[]{:S(2)}) async-start(bf16[8,2,80,2048]{3,2,1,0:T(8,128)(2,1)} %fusion.8), calls=%async_computation.3 | async-start | bytes 10485760 | tf_op jit(solution)/shard_map/all_to_all | solution.py:68
  583.5 4.7 copy-start.2
  587.1 12.4 %copy-start.1 = (bf16[2,384,2048]{2,1,0:T(8,128)(2,1)S(1)}, bf16[2,384,2048]{2,1,0:T(8,128)(2,1)}, u32[]{:S(2)}) copy-start(bf16[2,384,2048]{2,1,0:T(8,128)(2,1)} %param.13) | copy-start | bytes 9437188
Sparse Core Ops, SparseCore 0:
  341.3 79.0 reduce-scatter.1
